TPU v7x, 128 devices: a whole 4x4x4 slice. The times are simulated.
128 devices in a mesh: row: 16 (over z_hi, y, core), col: 8 (over z_lo, x).
Axes of the slice: x: 4, y: 4, z: 4 (z_hi: 2, z_lo: 2; z = z_hi * 2 + z_lo), core: 2. Of those that a mesh axis runs over, the one named last changes fastest.
Arguments:
- parent_inverse: float32 [24576, 24576], P('row', 'col'), may hold values from -6 to 6
- panel: float32 [24576, 1024], P(('col', 'row')), may hold values from -0.0390625 to 0.0390625
- saved_diag: float32 [1024, 1024], P('row', 'col'), may hold values from -6 to 6
Outputs:
- offdiag_block: float32 [24576, 1024], P(('row', 'col'))
- diag_block: float32 [1024, 1024], P('row', 'col')
All inputs are finite; a program needn't handle non-finite values.
Results may differ from a plain program's by a relative error of at most 0.00007.
Values sent between devices are 32-bit elements; how exact they have to be, the bound alone decides.
A program may use at most 128 MiB of HBM per device.

v0:
```python
import jax
import jax.numpy as jnp
from jax import lax
from jax.sharding import PartitionSpec as P


def spread(block, axis, holder):
    block = jnp.where(lax.axis_index(axis) == holder, block, jnp.zeros_like(block))
    return lax.psum(block, axis)


def shards(parent_inverse, panel, saved_diag):
    block_rows = parent_inverse.shape[0]
    column_count = lax.axis_size("col")
    keep_rows = block_rows // column_count
    column_panel = lax.all_gather(panel, "row", axis=0, tiled=True)
    row_index = lax.axis_index("row")
    column_index = lax.axis_index("col")
    local_half = lax.dynamic_slice_in_dim(column_panel, row_index % 2 * block_rows, block_rows, 0)
    product = lax.psum_scatter(
        jnp.dot(
            parent_inverse,
            column_panel,
            precision=lax.Precision.HIGHEST,
            preferred_element_type=jnp.float32,
        ),
        "col",
        scatter_dimension=0,
        tiled=True,
    )
    panel_half = spread(local_half, "col", row_index // 2)
    own_rows = lax.dynamic_slice_in_dim(panel_half, column_index * keep_rows, keep_rows, 0)
    offdiag_block = -product
    partial_value = lax.dot_general(
        own_rows,
        product,
        (((0,), (0,)), ((), ())),
        precision=lax.Precision.HIGHEST,
        preferred_element_type=jnp.float32,
    )
    by_columns = lax.psum_scatter(partial_value, "col", scatter_dimension=1, tiled=True)
    summed = lax.psum_scatter(by_columns, "row", scatter_dimension=0, tiled=True)
    diag_block = saved_diag + summed
    return (offdiag_block, diag_block)


def solution(mesh):
    in_specs = (P("row", "col"), P(("col", "row"), None), P("row", "col"))
    out_specs = (P(("row", "col"), None), P("row", "col"))
    return jax.shard_map(shards, mesh=mesh, in_specs=in_specs, out_specs=out_specs, check_vma=False)
```

profile of v0, /device:TPU:0, one launch (start us, length us, event | category | flops | bytes accessed | tf_op | source)
XLA Modules:
  0.0 462.0 jit_solution(5138972015593387433)
XLA Ops:
  7.2 0.0 all-gather.2.cloned.1.call-start
  7.2 0.7 all-gather.2.cloned.1.call-update
  7.9 0.0 all-reduce.2.cloned.1.call-start
  8.0 95.5 %all-gather.2.cloned.1.call-done = f32[3072,1024]{1,0:T(8,128)} async-done(((f32[192,1024]{1,0:T(8,128)}), f32[3072,1024]{1,0:T(8,128)}) %all-gather.2.cloned.1.call-update) | async-done | bytes 12582928 | tf_op jit(solution)/shard_map/all_gather | solution.py:16
  103.4 6.8 %dynamic-slice_select_fusion = f32[1536,1024]{1,0:T(8,128)} fusion(f32[3072,1024]{1,0:T(8,128)} %all-gather.2.cloned.1.call-done, s32[]{:T(128)S(6)} %select_n.28, pred[]{:T(512)S(6)} %eq.5), kind=kLoop, calls=%fused_computation | loop fusion | flops 1572864 | bytes 12582917 | tf_op jit(solution)/shard_map/jit(_where)/select_n | solution.py:8
  110.2 0.0 all-reduce.2.cloned.1.call-update
  110.2 0.0 reduce-scatter.4.cloned.1.call-start
  110.3 66.9 %fusion.3 = f32[1536,1024]{1,0:T(8,128)} fusion(f32[1536,3072]{1,0:T(8,128)} %param.3, f32[3072,1024]{1,0:T(8,128)} %all-gather.2.cloned.1.call-done), kind=kOutput, calls=%fused_computation.4 | convolution fusion | flops 57982058496 | bytes 37748736 | tf_op jit(solution)/shard_map/dot_general | solution.py:21
  177.2 0.0 reduce-scatter.4.cloned.1.call-update
  177.2 0.0 copy-start.1
  177.2 0.2 reduce-scatter.6.cloned.1.call-start
  177.5 75.2 %all-reduce.2.cloned.1.call-done = f32[1536,1024]{1,0:T(8,128)} async-done(((f32[1536,1024]{1,0:T(8,128)}), f32[1536,1024]{1,0:T(8,128)}) %all-reduce.2.cloned.1.call-update) | async-done | bytes 6291472 | tf_op jit(solution)/shard_map/psum | solution.py:9
  252.7 74.2 %reduce-scatter.4.cloned.1.call-done = f32[192,1024]{1,0:T(8,128)} async-done(((f32[1536,1024]{1,0:T(8,128)}), f32[192,1024]{1,0:T(8,128)}) %reduce-scatter.4.cloned.1.call-update) | async-done | bytes 786448 | tf_op jit(solution)/shard_map/reduce_scatter | solution.py:20
  326.9 0.0 copy-start
  326.9 6.9 %fusion = f32[1024,1024]{1,0:T(8,128)} fusion(f32[192,1024]{1,0:T(8,128)} %reduce-scatter.4.cloned.1.call-done, f32[1536,1024]{1,0:T(8,128)} %all-reduce.2.cloned.1.call-done, s32[]{:T(128)S(6)} %select_n.30), kind=kOutput, calls=%fused_computation.1 | convolution fusion | flops 2415919104 | bytes 5767172 | tf_op jit(solution)/shard_map/dot_general | solution.py:34
  333.8 0.0 reduce-scatter.6.cloned.1.call-update
  333.8 0.0 reduce-scatter.8.cloned.1.call-start
  333.9 52.0 %reduce-scatter.6.cloned.1.call-done = f32[1024,128]{1,0:T(8,128)} async-done(((f32[1024,1024]{1,0:T(8,128)}), f32[1024,128]{1,0:T(8,128)}) %reduce-scatter.6.cloned.1.call-update) | async-done | bytes 524304 | tf_op jit(solution)/shard_map/reduce_scatter | solution.py:41
  385.9 0.0 reduce-scatter.8.cloned.1.call-update
  385.9 0.0 copy-done
  385.9 0.9 neg.3
  386.9 67.3 %reduce-scatter.8.cloned.1.call-done = f32[64,128]{1,0:T(8,128)} async-done(((f32[1024,128]{1,0:T(8,128)}), f32[64,128]{1,0:T(8,128)}) %reduce-scatter.8.cloned.1.call-update) | async-done | bytes 32784 | tf_op jit(solution)/shard_map/reduce_scatter | solution.py:42
  454.1 0.0 copy-done.1
  454.1 1.4 add.25
Async XLA Ops:
  7.2 96.3 %all-gather.2.cloned.1.call-start = ((), (), s32[]{:S(2)}) async-start(), calls=%async_computation.3 | async-start | bytes 13369344 | tf_op jit(solution)/shard_map/all_gather | solution.py:16
  7.9 244.8 %all-reduce.2.cloned.1.call-start = ((), (), s32[]{:S(2)}) async-start(), calls=%async_computation.5 | async-start | bytes 12582912 | tf_op jit(solution)/shard_map/psum | solution.py:9
  110.2 216.7 %reduce-scatter.4.cloned.1.call-start = ((), (), s32[]{:S(2)}) async-start(), calls=%async_computation.4 | async-start | bytes 7077888 | tf_op jit(solution)/shard_map/reduce_scatter | solution.py:20
  177.2 276.9 %copy-start.1 = (f32[64,128]{1,0:T(8,128)S(1)}, f32[64,128]{1,0:T(8,128)}, u32[]{:S(2)}) copy-start(f32[64,128]{1,0:T(8,128)} %param.5) | copy-start | bytes 98308
  177.2 208.7 %reduce-scatter.6.cloned.1.call-start = ((), (), s32[]{:S(2)}) async-start(), calls=%async_computation.6 | async-start | bytes 4718592 | tf_op jit(solution)/shard_map/reduce_scatter | solution.py:41
  326.9 59.0 %copy-start = (f32[192,1024]{1,0:T(8,128)S(1)}, f32[192,1024]{1,0:T(8,128)}, u32[]{:S(2)}) copy-start(f32[192,1024]{1,0:T(8,128)} %reduce-scatter.4.cloned.1.call-done) | copy-start | bytes 2359300
  333.8 120.3 %reduce-scatter.8.cloned.1.call-start = ((), (), s32[]{:S(2)}) async-start(), calls=%async_computation.7 | async-start | bytes 557056 | tf_op jit(solution)/shard_map/reduce_scatter | solution.py:42
Sparse Core Ops, SparseCore 0:
  10.4 92.9 all-gather.1
  110.3 142.3 all-reduce.1
  255.1 71.7 reduce-scatter.3
  334.0 51.8 reduce-scatter.5
  389.5 64.5 reduce-scatter.7
where the time goes:
time: 462 us
  waiting for transfers between devices  365 us (79%)
  matrix products  73.8 us (16%)
  between operations  13.8 us (3%)
  other arithmetic  9.07 us (2%)
    all_gather x1, waiting for transfers between devices, shards(): column_panel = lax.all_gather(panel, 'row', axis=0, tiled=True)  95.5 us
    psum x1, waiting for transfers between devices, spread(): return lax.psum(block, axis)  75.2 us
    reduce_scatter x1, waiting for transfers between devices, shards(): lax.psum_scatter(jnp.dot(parent_inverse, column_panel, precision=lax.Prec...  74.2 us
    reduce_scatter x1, waiting for transfers between devices, shards(): lax.psum_scatter(by_columns, 'row', scatter_dimension=0, tiled=True)  67.3 us
    dot_general x1, matrix products, shards(): jnp.dot(parent_inverse, column_panel, precision=lax.Precision.HIGHEST, pr...  66.9 us
    reduce_scatter x1, waiting for transfers between devices, shards(): lax.psum_scatter(partial_value, 'col', scatter_dimension=1, tiled=True)  52 us
  transfers between devices with their start and end apart: 5, of which 5 were waited for; matrix products, arithmetic and copies ran while one was open for 15% of the time, Pallas kernels for 0%

commit v1 on v0

--- a/solution.py
+++ b/solution.py
@@ -6,7 +6,7 @@
 
 def spread(block, axis, holder):
     block = jnp.where(lax.axis_index(axis) == holder, block, jnp.zeros_like(block))
-    return lax.psum(block, axis)
+    return jnp.sum(lax.all_gather(block, axis), axis=0)
 
 
 def shards(parent_inverse, panel, saved_diag):

time: 462 us -> 803 us (1.74)
  waiting for transfers between devices: 365 us -> 684 us
  other arithmetic: 9.07 us -> 30.6 us
    all_gather x0 -> x1, waiting for transfers between devices: none -> 416 us  [spread(): return jnp.sum(lax.all_gather(block, axis), axis=0)]
    psum x1 -> x0, waiting for transfers between devices: 75.2 us -> none  [spread(): return lax.psum(block, axis)]
    reduce_scatter x1, waiting for transfers between devices: 74.2 us -> 52.6 us  [shards(): lax.psum_scatter(jnp.dot(parent_inverse, column_panel, precision=lax.Prec...]
    reduce_sum x0 -> x1, other arithmetic: none -> 21.5 us  [spread(): return jnp.sum(lax.all_gather(block, axis), axis=0)]
  transfers between devices with their start and end apart: 5 -> 5, of which waited for: 5 -> 5; matrix products, arithmetic and copies ran while one was open for 15% -> 11% of each run, Pallas kernels for 0% -> 0%
where the time goes in v1:
time: 803 us; the launch traced here: 802 us
  waiting for transfers between devices  684 us (85%)
  matrix products  73.7 us (9%)
  other arithmetic  30.6 us (4%)
  between operations  13.8 us (2%)
    all_gather x1, waiting for transfers between devices, spread(): return jnp.sum(lax.all_gather(block, axis), axis=0)  416 us
    all_gather x1, waiting for transfers between devices, shards(): column_panel = lax.all_gather(panel, 'row', axis=0, tiled=True)  95.5 us
    reduce_scatter x1, waiting for transfers between devices, shards(): lax.psum_scatter(by_columns, 'row', scatter_dimension=0, tiled=True)  67.3 us
    dot_general x1, matrix products, shards(): jnp.dot(parent_inverse, column_panel, precision=lax.Precision.HIGHEST, pr...  66.8 us
    reduce_scatter x1, waiting for transfers between devices, shards(): lax.psum_scatter(jnp.dot(parent_inverse, column_panel, precision=lax.Prec...  52.6 us
    reduce_scatter x1, waiting for transfers between devices, shards(): lax.psum_scatter(partial_value, 'col', scatter_dimension=1, tiled=True)  52 us
    reduce_sum x1, other arithmetic, spread(): return jnp.sum(lax.all_gather(block, axis), axis=0)  21.5 us
  transfers between devices with their start and end apart: 5, of which 5 were waited for; matrix products, arithmetic and copies ran while one was open for 11% of the time, Pallas kernels for 0%

profile of v1, /device:TPU:0, one launch (start us, length us, event | category | flops | bytes accessed | tf_op | source)
XLA Modules:
  0.0 802.2 jit_solution(12178304950509651453)
XLA Ops:
  7.2 0.0 all-gather.4.cloned.1.call-start
  7.2 0.7 all-gather.4.cloned.1.call-update
  7.9 0.0 all-gather.6.cloned.1.call-start
  8.0 95.5 %all-gather.4.cloned.1.call-done = f32[3072,1024]{1,0:T(8,128)} async-done(((f32[192,1024]{1,0:T(8,128)}), f32[3072,1024]{1,0:T(8,128)}) %all-gather.4.cloned.1.call-update) | async-done | bytes 12582928 | tf_op jit(solution)/shard_map/all_gather | solution.py:16
  103.4 6.7 dynamic-slice_select_fusion
  110.2 0.0 all-gather.6.cloned.1.call-update
  110.2 0.0 reduce-scatter.4.cloned.1.call-start
  110.3 66.8 %fusion.3 = f32[1536,1024]{1,0:T(8,128)} fusion(f32[1536,3072]{1,0:T(8,128)} %param.3, f32[3072,1024]{1,0:T(8,128)} %all-gather.4.cloned.1.call-done), kind=kOutput, calls=%fused_computation.4 | convolution fusion | flops 57982058496 | bytes 37748736 | tf_op jit(solution)/shard_map/dot_general | solution.py:21
  177.1 0.0 reduce-scatter.4.cloned.1.call-update
  177.1 0.2 reduce-scatter.6.cloned.1.call-start
  177.3 415.7 %all-gather.6.cloned.1.call-done = f32[12288,1024]{1,0:T(8,128)} async-done(((f32[1536,1024]{1,0:T(8,128)}), f32[12288,1024]{1,0:T(8,128)}) %all-gather.6.cloned.1.call-update) | async-done | bytes 50331664 | tf_op jit(solution)/shard_map/all_gather | solution.py:9
  593.0 21.5 %reduce_sum.9 = f32[1536,1024]{1,0:T(8,128)} reduce(f32[8,1536,1024]{2,1,0:T(8,128)} %bitcast.4, f32[]{:T(128)} %constant.41.clone.1), dimensions={0}, to_apply=%region_1.2 | reduce | flops 11010048 | bytes 56623108 | tf_op jit(solution)/shard_map/reduce_sum | solution.py:9
  614.5 0.0 copy-start.1
  614.5 52.6 %reduce-scatter.4.cloned.1.call-done = f32[192,1024]{1,0:T(8,128)} async-done(((f32[1536,1024]{1,0:T(8,128)}), f32[192,1024]{1,0:T(8,128)}) %reduce-scatter.4.cloned.1.call-update) | async-done | bytes 786448 | tf_op jit(solution)/shard_map/reduce_scatter | solution.py:20
  667.1 0.0 copy-start
  667.1 6.9 fusion
  674.0 0.0 reduce-scatter.6.cloned.1.call-update
  674.0 0.0 reduce-scatter.8.cloned.1.call-start
  674.1 52.0 %reduce-scatter.6.cloned.1.call-done = f32[1024,128]{1,0:T(8,128)} async-done(((f32[1024,1024]{1,0:T(8,128)}), f32[1024,128]{1,0:T(8,128)}) %reduce-scatter.6.cloned.1.call-update) | async-done | bytes 524304 | tf_op jit(solution)/shard_map/reduce_scatter | solution.py:41
  726.1 0.0 reduce-scatter.8.cloned.1.call-update
  726.1 0.0 copy-done
  726.1 0.9 neg.3
  727.0 67.3 %reduce-scatter.8.cloned.1.call-done = f32[64,128]{1,0:T(8,128)} async-done(((f32[1024,128]{1,0:T(8,128)}), f32[64,128]{1,0:T(8,128)}) %reduce-scatter.8.cloned.1.call-update) | async-done | bytes 32784 | tf_op jit(solution)/shard_map/reduce_scatter | solution.py:42
  794.3 0.0 copy-done.1
  794.3 1.4 add.23
Async XLA Ops:
  7.2 96.3 %all-gather.4.cloned.1.call-start = ((), (), s32[]{:S(2)}) async-start(), calls=%async_computation.3 | async-start | bytes 13369344 | tf_op jit(solution)/shard_map/all_gather | solution.py:16
  7.9 585.1 %all-gather.6.cloned.1.call-start = ((), (), s32[]{:S(2)}) async-start(), calls=%async_computation.7 | async-start | bytes 56623104 | tf_op jit(solution)/shard_map/all_gather | solution.py:9
  110.2 556.9 %reduce-scatter.4.cloned.1.call-start = ((), (), s32[]{:S(2)}) async-start(), calls=%async_computation.4 | async-start | bytes 7077888 | tf_op jit(solution)/shard_map/reduce_scatter | solution.py:20
  177.1 549.0 %reduce-scatter.6.cloned.1.call-start = ((), (), s32[]{:S(2)}) async-start(), calls=%async_computation.5 | async-start | bytes 4718592 | tf_op jit(solution)/shard_map/reduce_scatter | solution.py:41
  614.5 179.8 %copy-start.1 = (f32[64,128]{1,0:T(8,128)S(1)}, f32[64,128]{1,0:T(8,128)}, u32[]{:S(2)}) copy-start(f32[64,128]{1,0:T(8,128)} %param.5) | copy-start | bytes 98308
  667.1 59.0 %copy-start = (f32[192,1024]{1,0:T(8,128)S(1)}, f32[192,1024]{1,0:T(8,128)}, u32[]{:S(2)}) copy-start(f32[192,1024]{1,0:T(8,128)} %reduce-scatter.4.cloned.1.call-done) | copy-start | bytes 2359300
  674.0 120.3 %reduce-scatter.8.cloned.1.call-start = ((), (), s32[]{:S(2)}) async-start(), calls=%async_computation.6 | async-start | bytes 557056 | tf_op jit(solution)/shard_map/reduce_scatter | solution.py:42
Sparse Core Ops, SparseCore 0:
  10.4 92.9 all-gather.3
  110.3 482.6 all-gather.5
  595.4 71.6 reduce-scatter.3
  674.1 51.8 reduce-scatter.5
  729.7 64.5 reduce-scatter.7

commit v2 on v0

--- a/solution.py
+++ b/solution.py
@@ -13,7 +13,9 @@
     block_rows = parent_inverse.shape[0]
     column_count = lax.axis_size("col")
     keep_rows = block_rows // column_count
-    column_panel = lax.all_gather(panel, "row", axis=0, tiled=True)
+    column_panel = jnp.concatenate(
+        lax.all_to_all(jnp.stack([panel] * lax.axis_size("row")), "row", 0, 0), axis=0
+    )
     row_index = lax.axis_index("row")
     column_index = lax.axis_index("col")
     local_half = lax.dynamic_slice_in_dim(column_panel, row_index % 2 * block_rows, block_rows, 0)

time: 462 us -> 553 us (1.20)
  waiting for transfers between devices: 365 us -> 441 us
  starting transfers between devices: 0.38 us -> 8.39 us
  local copies, waits for them, and re-layouts: 0.01 us -> 7.22 us
    all_to_all x0 -> x1, waiting for transfers between devices: none -> 169 us  [shards(): lax.all_to_all(jnp.stack([panel] * lax.axis_size('row')), 'row', 0, 0)]
    all_gather x1 -> x0, waiting for transfers between devices: 95.5 us -> none  [shards(): column_panel = lax.all_gather(panel, 'row', axis=0, tiled=True)]
    all_to_all x0 -> x1, starting transfers between devices: none -> 8.04 us  [shards(): lax.all_to_all(jnp.stack([panel] * lax.axis_size('row')), 'row', 0, 0)]
    another operation x0 -> x1, local copies, waits for them, and re-layouts: none -> 7.21 us  [shards(): jnp.stack([panel] * lax.axis_size('row'))]
  transfers between devices with their start and end apart: 5 -> 5, of which waited for: 5 -> 5; matrix products, arithmetic and copies ran while one was open for 15% -> 12% of each run, Pallas kernels for 0% -> 0%
where the time goes in v2:
time: 553 us
  waiting for transfers between devices  441 us (80%)
  matrix products  73.8 us (13%)
  between operations  13.8 us (2%)
  other arithmetic  9.05 us (2%)
  starting transfers between devices  8.39 us (2%)
  local copies, waits for them, and re-layouts  7.22 us (1%)
    all_to_all x1, waiting for transfers between devices, shards(): lax.all_to_all(jnp.stack([panel] * lax.axis_size('row')), 'row', 0, 0)  169 us
    psum x1, waiting for transfers between devices, spread(): return lax.psum(block, axis)  78.4 us
    reduce_scatter x1, waiting for transfers between devices, shards(): lax.psum_scatter(jnp.dot(parent_inverse, column_panel, precision=lax.Prec...  74.2 us
    reduce_scatter x1, waiting for transfers between devices, shards(): lax.psum_scatter(by_columns, 'row', scatter_dimension=0, tiled=True)  67.3 us
    dot_general x1, matrix products, shards(): jnp.dot(parent_inverse, column_panel, precision=lax.Precision.HIGHEST, pr...  66.9 us
    reduce_scatter x1, waiting for transfers between devices, shards(): lax.psum_scatter(partial_value, 'col', scatter_dimension=1, tiled=True)  52 us
  transfers between devices with their start and end apart: 5, of which 5 were waited for; matrix products, arithmetic and copies ran while one was open for 12% of the time, Pallas kernels for 0%

profile of v2, /device:TPU:0, one launch (start us, length us, event | category | flops | bytes accessed | tf_op | source)
XLA Modules:
  0.0 553.0 jit_solution(13162477384150216974)
XLA Ops:
  7.2 7.2 %stack.2 = f32[16,192,1024]{2,1,0:T(8,128)} broadcast(f32[192,1024]{1,0:T(8,128)} %param.4), dimensions={1,2} | broadcast | bytes 13369344 | tf_op jit(solution)/shard_map/stack | solution.py:17
  14.4 8.0 %all-to-all-start = ((f32[16,192,1024]{2,1,0:T(8,128)}), f32[16,192,1024]{2,1,0:T(8,128)}, u32[]{:S(2)}, u32[]{:S(2)}) async-start(f32[16,192,1024]{2,1,0:T(8,128)} %stack.2), calls=%async_computation | async-start | bytes 25165824 | tf_op jit(solution)/shard_map/all_to_all | solution.py:17
  22.4 0.0 all-reduce.2.cloned.1.call-start
  22.5 168.8 %all-to-all-done = f32[16,192,1024]{2,1,0:T(8,128)} async-done(((f32[16,192,1024]{2,1,0:T(8,128)}), f32[16,192,1024]{2,1,0:T(8,128)}, u32[]{:S(2)}, u32[]{:S(2)}) %all-to-all-start) | async-done | bytes 12582944 | tf_op jit(solution)/shard_map/all_to_all | solution.py:17
  191.3 6.7 %dynamic-slice_select_fusion = f32[1536,1024]{1,0:T(8,128)} fusion(f32[3072,1024]{1,0:T(8,128)} %bitcast, s32[]{:T(128)S(6)} %select_n.28, pred[]{:T(512)S(6)} %eq.5), kind=kLoop, calls=%fused_computation | loop fusion | flops 1572864 | bytes 12582917 | tf_op jit(solution)/shard_map/jit(_where)/select_n | solution.py:8
  198.0 0.0 all-reduce.2.cloned.1.call-update
  198.0 0.0 reduce-scatter.4.cloned.1.call-start
  198.1 66.9 %fusion.3 = f32[1536,1024]{1,0:T(8,128)} fusion(f32[1536,3072]{1,0:T(8,128)} %param.3, f32[3072,1024]{1,0:T(8,128)} %bitcast), kind=kOutput, calls=%fused_computation.4 | convolution fusion | flops 57982058496 | bytes 37748736 | tf_op jit(solution)/shard_map/dot_general | solution.py:23
  265.0 0.0 reduce-scatter.4.cloned.1.call-update
  265.0 0.0 copy-start.1
  265.1 0.2 reduce-scatter.6.cloned.1.call-start
  265.3 78.4 %all-reduce.2.cloned.1.call-done = f32[1536,1024]{1,0:T(8,128)} async-done(((f32[1536,1024]{1,0:T(8,128)}), f32[1536,1024]{1,0:T(8,128)}) %all-reduce.2.cloned.1.call-update) | async-done | bytes 6291472 | tf_op jit(solution)/shard_map/psum | solution.py:9
  343.7 74.2 %reduce-scatter.4.cloned.1.call-done = f32[192,1024]{1,0:T(8,128)} async-done(((f32[1536,1024]{1,0:T(8,128)}), f32[192,1024]{1,0:T(8,128)}) %reduce-scatter.4.cloned.1.call-update) | async-done | bytes 786448 | tf_op jit(solution)/shard_map/reduce_scatter | solution.py:22
  417.9 0.0 copy-start
  417.9 6.9 %fusion = f32[1024,1024]{1,0:T(8,128)} fusion(f32[192,1024]{1,0:T(8,128)} %reduce-scatter.4.cloned.1.call-done, f32[1536,1024]{1,0:T(8,128)} %all-reduce.2.cloned.1.call-done, s32[]{:T(128)S(6)} %select_n.30), kind=kOutput, calls=%fused_computation.1 | convolution fusion | flops 2415919104 | bytes 5767172 | tf_op jit(solution)/shard_map/dot_general | solution.py:36
  424.8 0.0 reduce-scatter.6.cloned.1.call-update
  424.8 0.0 reduce-scatter.8.cloned.1.call-start
  424.9 52.0 %reduce-scatter.6.cloned.1.call-done = f32[1024,128]{1,0:T(8,128)} async-done(((f32[1024,1024]{1,0:T(8,128)}), f32[1024,128]{1,0:T(8,128)}) %reduce-scatter.6.cloned.1.call-update) | async-done | bytes 524304 | tf_op jit(solution)/shard_map/reduce_scatter | solution.py:43
  476.9 0.0 reduce-scatter.8.cloned.1.call-update
  476.9 0.0 copy-done
  476.9 0.9 neg.3
  477.8 67.3 %reduce-scatter.8.cloned.1.call-done = f32[64,128]{1,0:T(8,128)} async-done(((f32[1024,128]{1,0:T(8,128)}), f32[64,128]{1,0:T(8,128)}) %reduce-scatter.8.cloned.1.call-update) | async-done | bytes 32784 | tf_op jit(solution)/shard_map/reduce_scatter | solution.py:44
  545.1 0.0 copy-done.1
  545.1 1.4 add.25
Async XLA Ops:
  14.4 176.9 %all-to-all-start = ((f32[16,192,1024]{2,1,0:T(8,128)}), f32[16,192,1024]{2,1,0:T(8,128)}, u32[]{:S(2)}, u32[]{:S(2)}) async-start(f32[16,192,1024]{2,1,0:T(8,128)} %stack.2), calls=%async_computation | async-start | bytes 25165824 | tf_op jit(solution)/shard_map/all_to_all | solution.py:17
  22.4 321.3 %all-reduce.2.cloned.1.call-start = ((), (), s32[]{:S(2)}) async-start(), calls=%async_computation.5 | async-start | bytes 12582912 | tf_op jit(solution)/shard_map/psum | solution.py:9
  198.0 219.9 %reduce-scatter.4.cloned.1.call-start = ((), (), s32[]{:S(2)}) async-start(), calls=%async_computation.4 | async-start | bytes 7077888 | tf_op jit(solution)/shard_map/reduce_scatter | solution.py:22
  265.0 280.1 %copy-start.1 = (f32[64,128]{1,0:T(8,128)S(1)}, f32[64,128]{1,0:T(8,128)}, u32[]{:S(2)}) copy-start(f32[64,128]{1,0:T(8,128)} %param.5) | copy-start | bytes 98308
  265.1 211.8 %reduce-scatter.6.cloned.1.call-start = ((), (), s32[]{:S(2)}) async-start(), calls=%async_computation.6 | async-start | bytes 4718592 | tf_op jit(solution)/shard_map/reduce_scatter | solution.py:43
  417.9 58.9 %copy-start = (f32[192,1024]{1,0:T(8,128)S(1)}, f32[192,1024]{1,0:T(8,128)}, u32[]{:S(2)}) copy-start(f32[192,1024]{1,0:T(8,128)} %reduce-scatter.4.cloned.1.call-done) | copy-start | bytes 2359300
  424.8 120.3 %reduce-scatter.8.cloned.1.call-start = ((), (), s32[]{:S(2)}) async-start(), calls=%async_computation.7 | async-start | bytes 557056 | tf_op jit(solution)/shard_map/reduce_scatter | solution.py:44
Sparse Core Ops, SparseCore 0:
  198.2 145.4 all-reduce.1
  346.1 71.7 reduce-scatter.3
  425.0 51.8 reduce-scatter.5
  480.5 64.6 reduce-scatter.7
